TPU v7x, 256 devices: a whole 4x4x8 slice. The times are simulated.
256 devices in a mesh: ctx: 32 (over z_hi, y, x), ch: 8 (over z_lo, core).
Axes of the slice: x: 4, y: 4, z: 8 (z_hi: 2, z_lo: 4; z = z_hi * 4 + z_lo), core: 2. Of those that a mesh axis runs over, the one named last changes fastest.
Arguments:
- grad_out: bfloat16 [24576, 4096], P('ctx', 'ch'), may hold values from -6 to 6
- block_input: bfloat16 [24576, 4096], P('ctx', 'ch'), may hold values from -40 to 40
- norm_gain: bfloat16 [4096], P('ch'), may hold values from 0.5 to 1.5
- queries: bfloat16 [24576, 4096], P('ctx', 'ch'), may hold values from -6 to 6
- keys: bfloat16 [24576, 4096], P('ctx', 'ch'), may hold values from -6 to 6
- values: bfloat16 [24576, 4096], P('ctx', 'ch'), may hold values from -6 to 6
- filters: bfloat16 [256, 128], P('ch'), may hold values from -0.5 to 0.5
- doc_starts: int32 [32, 4], P('ctx'), may hold values from 0 to 767, as said below
- in_weight: bfloat16 [4096, 3, 4096], P('ctx', None, 'ch'), may hold values from -0.09375 to 0.09375
- out_weight: bfloat16 [4096, 4096], P('ch', 'ctx'), may hold values from -0.09375 to 0.09375
Outputs:
- grad_input: bfloat16 [24576, 4096], P('ctx', 'ch')
Inputs may be any that keep to these rules, and one draw needn't show every extreme that they name: `doc_starts`: each row holds 4 distinct document starts of one slab as offsets within the slab, in ascending order; the first slab's first start is 0.
All inputs are finite; a program needn't handle non-finite values.
Results may differ from a plain program's by a relative error of at most 0.013.
Values may be sent and summed in bfloat16 or wider, within the bound.
A program may use at most 128 MiB of HBM per device.

v0:
```python
import jax
import jax.numpy as jnp
from jax import lax
from jax.sharding import PartitionSpec as P

D = 4096
FILTER_LEN = 128
GROUP_WIDTH = 16
DOCS = 4


epsilon = 1e-05


def shifted(block, axis, distance):
    devices = range(lax.axis_size(axis))
    route = [(i - distance, i) for i in devices if i - distance in devices]
    return lax.ppermute(block, axis, route)


def on_device(
    grad_out,
    block_input,
    norm_gain,
    queries,
    keys,
    values,
    filters,
    doc_starts,
    in_weight,
    out_weight,
):
    tok_rows = grad_out.shape[0]
    chan_width = grad_out.shape[1]
    group_count = filters.shape[0]
    tile_count = tok_rows // FILTER_LEN
    source_in = block_input.astype(jnp.float32)
    square_sum = lax.psum(jnp.sum(source_in * source_in, axis=1), "ch")
    starts = doc_starts[0]
    positions = jnp.arange(tok_rows, dtype=jnp.int32)
    own_last = jnp.max(
        jnp.where(starts[None, :] <= positions[:, None], starts[None, :], -tok_rows), axis=1
    )
    products = (keys.astype(jnp.float32) * values.astype(jnp.float32)).astype(jnp.bfloat16)
    tail_rows, prior_start = shifted(
        (products[tok_rows - FILTER_LEN :], starts[DOCS - 1 :]), "ctx", 1
    )
    last_start = jnp.maximum(own_last, prior_start[0] - tok_rows)
    tap_index = (
        jnp.arange(FILTER_LEN, dtype=jnp.int32)[:, None]
        + FILTER_LEN
        - jnp.arange(2 * FILTER_LEN, dtype=jnp.int32)[None, :]
    )
    selector = (jnp.arange(FILTER_LEN, dtype=jnp.int32)[:, None, None] == tap_index[None]).astype(
        jnp.bfloat16
    )
    selector = selector.reshape(FILTER_LEN, 2 * FILTER_LEN * FILTER_LEN)
    table = jnp.dot(filters, selector, preferred_element_type=jnp.float32).astype(jnp.bfloat16)
    table = table.reshape(group_count, FILTER_LEN, 2 * FILTER_LEN)
    flipped = table[:, ::-1, ::-1]
    padded_prod = jnp.concatenate([tail_rows, products], axis=0)

    def forward_tile(tile_idx):
        source = lax.dynamic_slice_in_dim(padded_prod, tile_idx * FILTER_LEN, 2 * FILTER_LEN, 0)
        source = source.reshape(2 * FILTER_LEN, group_count, GROUP_WIDTH)
        row_last = lax.dynamic_slice_in_dim(last_start, tile_idx * FILTER_LEN, FILTER_LEN, 0)
        col_pos = (tile_idx - 1) * FILTER_LEN + jnp.arange(2 * FILTER_LEN, dtype=jnp.int32)
        allowed = col_pos[None, :] >= row_last[:, None]
        masked = jnp.where(allowed[None], table, jnp.zeros_like(table))
        return jnp.einsum(
            "gtp,pgc->tgc", masked, source, preferred_element_type=jnp.float32
        ).reshape(FILTER_LEN, chan_width)

    mixed = lax.map(forward_tile, jnp.arange(tile_count, dtype=jnp.int32)).reshape(
        tok_rows, chan_width
    )
    gathered = lax.all_gather(grad_out, "ch", axis=1, tiled=True)
    mix_grad = lax.dot_general(
        gathered,
        lax.all_gather(out_weight, "ctx", axis=1, tiled=True),
        (((1,), (1,)), ((), ())),
        preferred_element_type=jnp.float32,
    )
    q_grad = (mix_grad * mixed).astype(jnp.bfloat16)
    w_grad = (mix_grad * queries.astype(jnp.float32)).astype(jnp.bfloat16)
    head_rows, head_last = shifted((w_grad[:FILTER_LEN], last_start[:FILTER_LEN]), "ctx", -1)
    padded_grad = jnp.concatenate([w_grad, head_rows], axis=0)
    padded_last = jnp.concatenate([last_start, head_last + tok_rows], axis=0)

    def backward_tile(tile_idx):
        source = lax.dynamic_slice_in_dim(padded_grad, tile_idx * FILTER_LEN, 2 * FILTER_LEN, 0)
        source = source.reshape(2 * FILTER_LEN, group_count, GROUP_WIDTH)
        col_last = lax.dynamic_slice_in_dim(padded_last, tile_idx * FILTER_LEN, 2 * FILTER_LEN, 0)
        row_pos = tile_idx * FILTER_LEN + jnp.arange(FILTER_LEN, dtype=jnp.int32)
        allowed = row_pos[:, None] >= col_last[None, :]
        masked = jnp.where(allowed[None], flipped, jnp.zeros_like(flipped))
        return jnp.einsum(
            "gst,tgc->sgc", masked, source, preferred_element_type=jnp.float32
        ).reshape(FILTER_LEN, chan_width)

    conv_grad = lax.map(backward_tile, jnp.arange(tile_count, dtype=jnp.int32)).reshape(
        tok_rows, chan_width
    )
    k_grad = (conv_grad * values.astype(jnp.float32)).astype(jnp.bfloat16)
    v_grad = (conv_grad * keys.astype(jnp.float32)).astype(jnp.bfloat16)
    stacked = jnp.stack([q_grad, k_grad, v_grad], axis=1).reshape(tok_rows, 3 * chan_width)
    weight_rows = lax.all_gather(in_weight, "ctx", axis=0, tiled=True)
    flat_rows = weight_rows.reshape(weight_rows.shape[0], 3 * chan_width)
    hidden_terms = lax.dot_general(
        stacked, flat_rows, (((1,), (1,)), ((), ())), preferred_element_type=jnp.float32
    )
    norm_grad = lax.psum_scatter(
        hidden_terms.astype(jnp.bfloat16), "ch", scatter_dimension=1, tiled=True
    ).astype(jnp.float32)
    scaled = norm_gain.astype(jnp.float32)[None, :] * norm_grad
    cross_sum = lax.psum(jnp.sum(scaled * source_in, axis=1), "ch")
    inverse = lax.rsqrt(square_sum / D + epsilon)[:, None]
    result = (
        grad_out.astype(jnp.float32)
        + inverse * scaled
        - source_in * (inverse * inverse * inverse) * cross_sum[:, None] / D
    )
    return result.astype(jnp.bfloat16)


def solution(mesh):
    placed = (
        P("ctx", "ch"),
        P("ctx", "ch"),
        P("ch"),
        P("ctx", "ch"),
        P("ctx", "ch"),
        P("ctx", "ch"),
        P("ch", None),
        P("ctx", None),
        P("ctx", None, "ch"),
        P("ch", "ctx"),
    )
    return jax.shard_map(
        on_device, mesh=mesh, in_specs=placed, out_specs=P("ctx", "ch"), check_vma=False
    )
```

profile of v0, /device:TPU:1, one launch (start us, length us, event | category | flops | bytes accessed | tf_op | source)
XLA Modules:
  0.0 529.9 jit_solution(16419598484490058867)
XLA Ops:
  8.8 1.3 fusion.17
  10.2 3.9 collective-permute-start
  14.7 3.6 collective-permute-start.1
  18.7 3.5 convolution_convert_fusion
  22.7 22.6 %rev.3 = bf16[32,128,256]{2,1,0:T(8,128)(2,1)} reverse(bf16[32,128,256]{2,1,0:T(8,128)(2,1)S(1)} %bitcast.57), dimensions={1,2} | reverse | bytes 4194304 | tf_op jit(solution)/shard_map/rev | solution.py:60
  46.0 1.3 collective-permute-start.3
  47.3 1.0 pad_maximum_fusion
  48.3 1.4 broadcast.91.clone2
  49.7 28.5 %while.22 = (s32[]{:T(128)}, f32[6,128,512]{2,1,0:T(8,128)}, s32[6]{0:T(128)S(1)}, bf16[896,512]{1,0:T(8,128)(2,1)}, s32[768]{0:T(1024)S(1)}, /*index=5*/bf16[32...) while((s32[]{:T(128)}, f32[6,128,512]{2,1,0:T(8,128)}, ...), condition=%wide.region_4.5_spmd, body=%wide.region_3.4_spmd.sunk | while | flops 34636040 | bytes 4788460 | solution.py:74
  51.8 1.0 constant_dynamic-slice_fusion.4
  56.5 1.0 constant_dynamic-slice_fusion.4
  61.3 1.0 constant_dynamic-slice_fusion.4
  75.5 1.0 constant_dynamic-slice_fusion.4
  78.2 68.1 %all-gather.6.cloned.1.call-done = bf16[512,4096]{1,0:T(8,128)(2,1)} async-done(((bf16[512,128]{1,0:T(8,128)(2,1)}), bf16[512,4096]{1,0:T(8,128)(2,1)}) %all-gather.6.cloned.1.call-update) | async-done | bytes 4194320 | tf_op jit(solution)/shard_map/all_gather | solution.py:80
  146.2 71.0 %all-gather.4.cloned.1.call-done = bf16[768,4096]{1,0:T(8,128)(2,1)} async-done(((bf16[768,512]{1,0:T(8,128)(2,1)}), bf16[768,4096]{1,0:T(8,128)(2,1)}) %all-gather.4.cloned.1.call-update) | async-done | bytes 6291472 | tf_op jit(solution)/shard_map/all_gather | solution.py:77
  217.3 9.0 %fusion.25 = (bf16[768,512]{1,0:T(8,128)(2,1)}, bf16[768,512]{1,0:T(8,128)(2,1)S(1)}) fusion(f32[6,128,512]{2,1,0:T(8,128)} %get-tuple-element.114, bf16[768,512]{1,0:T(8,128)(2,1)} %param.17, bf16[768,4096]{1,0:T(8,128)(2,1)} %all-gather.4.cloned.1.call-done, bf16[512,4096]{1,0:T(8,128)(2,1)} %all-gather.6.cloned.1.call-done), kind=kOutput, calls=%fused_computation.43 | convolution fusion | flops 3223191552 | bytes 14417920 | tf_op jit(solution)/shard_map/dot_general | solution.py:78
  226.3 1.5 collective-permute-start.2
  227.8 4.2 collective-permute-done.2
  232.2 23.9 %while.23 = (s32[]{:T(128)}, f32[6,128,512]{2,1,0:T(8,128)S(1)}, s32[6]{0:T(128)S(1)}, bf16[896,512]{1,0:T(8,128)(2,1)S(1)}, s32[896]{0:T(1024)S(1)}, /*index=5*...) while((s32[]{:T(128)}, f32[6,128,512]{2,1,0:T(8,128)S(1)}, s32[6]{0:T(128)S(1)}, ...), condition=%wide.region_6.7_spmd, body=%wide.region_5.6_spmd.sunk | while | flops 34635908 | bytes 4788399 | solution.py:101
  233.8 2.4 fusion.44
  237.8 2.2 fusion.44
  241.8 2.2 fusion.44
  245.7 2.2 fusion.44
  249.7 2.2 fusion.44
  253.7 2.2 fusion.44
  256.1 1.8 fusion.18
  257.9 163.2 %all-gather.8.cloned.1.call-done = bf16[4096,3,512]{2,0,1:T(8,128)(2,1)} async-done(((bf16[128,3,512]{2,0,1:T(8,128)(2,1)}), bf16[4096,3,512]{2,0,1:T(8,128)(2,1)}) %all-gather.8.cloned.1.call-update) | async-done | bytes 12582928 | tf_op jit(solution)/shard_map/all_gather | solution.py:107
  421.1 14.8 %bitcast_convert_fusion = bf16[768,4096]{1,0:T(8,128)(2,1)} fusion(bf16[4096,3,512]{2,0,1:T(8,128)(2,1)} %all-gather.8.cloned.1.call-done, bf16[768,1,512]{2,0,1:T(8,128)(2,1)S(1)} %bitcast.65, bf16[768,1,512]{2,0,1:T(8,128)(2,1)S(1)} %bitcast.64, bf16[768,1,512]{2,0,1:T(8,128)(2,1)} %bitcast.69), kind=kOutput, calls=%fused_computation.20 | convolution fusion | flops 9669181440 | bytes 21233664 | tf_op jit(solution)/shard_map/dot_general | solution.py:109
  436.5 67.7 %reduce-scatter.2.cloned.1.call-done = bf16[768,512]{1,0:T(8,128)(2,1)} async-done(((bf16[768,4096]{1,0:T(8,128)(2,1)}), bf16[768,512]{1,0:T(8,128)(2,1)}) %reduce-scatter.2.cloned.1.call-update) | async-done | bytes 786448 | tf_op jit(solution)/shard_map/reduce_scatter | solution.py:112
  504.3 1.6 fusion.19
  505.9 16.0 %all-reduce = (f32[768]{0:T(1024)S(1)}, f32[768]{0:T(1024)S(1)}) all-reduce(f32[768]{0:T(1024)S(1)} %get-tuple-element.141, f32[768]{0:T(1024)S(1)} %get-tuple-element.140), channel_id=1, replica_groups=mesh['ctx'=32,'ch'=8] {'ch'}, use_global_device_ids=true, to_apply=%region_9.10 | all-reduce | flops 1536 | bytes 12288 | tf_op jit(solution)/shard_map/psum | solution.py:116
  521.9 1.5 fusion.23
  (143 shorter events, 27.8 us)
Async XLA Ops:
  6.5 12.1 %copy-start = (bf16[32,128]{1,0:T(8,128)(2,1)S(1)}, bf16[32,128]{1,0:T(8,128)(2,1)}, u32[]{:S(2)}) copy-start(bf16[32,128]{1,0:T(8,128)(2,1)} %param.20) | copy-start | bytes 24580
  6.5 2.3 copy-start.1
  6.5 139.7 %all-gather.6.cloned.1.call-start = ((), (), s32[]{:S(2)}) async-start(), calls=%async_computation.2 | async-start | bytes 4325376 | tf_op jit(solution)/shard_map/all_gather | solution.py:80
  7.3 210.0 %all-gather.4.cloned.1.call-start = ((), (), s32[]{:S(2)}) async-start(), calls=%async_computation.1 | async-start | bytes 7077888 | tf_op jit(solution)/shard_map/all_gather | solution.py:77
  8.0 6.1 %copy-start.6 = (s32[1,4]{1,0:T(1,128)S(1)}, s32[1,4]{1,0:T(1,128)}, u32[]{:S(2)}) copy-start(s32[1,4]{1,0:T(1,128)} %param.21) | copy-start | bytes 52
  8.0 413.0 %all-gather.8.cloned.1.call-start = ((), (), s32[]{:S(2)}) async-start(), calls=%async_computation.3 | async-start | bytes 12976128 | tf_op jit(solution)/shard_map/all_gather | solution.py:107
  8.8 495.5 %reduce-scatter.2.cloned.1.call-start = ((), (), s32[]{:S(2)}) async-start(), calls=%async_computation.4 | async-start | bytes 7077888 | tf_op jit(solution)/shard_map/reduce_scatter | solution.py:112
  10.2 37.1 %collective-permute-start = (bf16[128,512]{1,0:T(8,128)(2,1)S(1)}, bf16[128,512]{1,0:T(8,128)(2,1)S(1)}, u32[]{:S(2)}, u32[]{:S(2)}) collective-permute-start(bf16[128,512]{1,0:T(8,128)(2,1)S(1)} %slice.20), channel_id=1, source_target_pairs={{0,8},{8,16},{16,24},{24,32},{32,40},{40,48},{48,56},{56,64},{64,7... | collective-permute-start | bytes 393224 | tf_op jit(solution)/shard_map/ppermute | solution.py:18
  14.7 30.6 %collective-permute-start.1 = (s32[1]{0:T(128)}, s32[1]{0:T(128)}, u32[]{:S(2)}, u32[]{:S(2)}) collective-permute-start(s32[1]{0:T(128)} %bitcast.10), channel_id=1, source_target_pairs={{0,8},{8,16},{16,24},{24,32},{32,40},{40,48},{48,56},{56,64},{64,7... | collective-permute-start | bytes 20 | tf_op jit(solution)/shard_map/ppermute | solution.py:18
  46.0 181.8 %collective-permute-start.3 = (s32[128]{0:T(128)S(1)}, s32[128]{0:T(128)S(1)}, u32[]{:S(2)}, u32[]{:S(2)}) collective-permute-start(s32[128]{0:T(128)S(1)} %slice.19), channel_id=1, source_target_pairs={{8,0},{16,8},{24,16},{32,24},{40,32},{48,40},{56,48},{64,56},{72,6... | collective-permute-start | bytes 1544 | tf_op jit(solution)/shard_map/ppermute | solution.py:18
  226.3 5.7 %collective-permute-start.2 = (bf16[128,512]{1,0:T(8,128)(2,1)S(1)}, bf16[128,512]{1,0:T(8,128)(2,1)S(1)}, u32[]{:S(2)}, u32[]{:S(2)}) collective-permute-start(bf16[128,512]{1,0:T(8,128)(2,1)S(1)} %slice.21), channel_id=1, source_target_pairs={{8,0},{16,8},{24,16},{32,24},{40,32},{48,40},{56,48},{64,56},{72,6... | collective-permute-start | bytes 393224 | tf_op jit(solution)/shard_map/ppermute | solution.py:18
  435.8 0.7 copy-start.5
  435.8 68.4 %copy-start.2 = (bf16[768,512]{1,0:T(8,128)(2,1)S(1)}, bf16[768,512]{1,0:T(8,128)(2,1)}, u32[]{:S(2)}) copy-start(bf16[768,512]{1,0:T(8,128)(2,1)} %param.15) | copy-start | bytes 2359300
  436.5 85.4 %copy-start.3 = (bf16[768,512]{1,0:T(8,128)(2,1)S(1)}, bf16[768,512]{1,0:T(8,128)(2,1)}, u32[]{:S(2)}) copy-start(bf16[768,512]{1,0:T(8,128)(2,1)} %param.14) | copy-start | bytes 2359300
  504.3 17.7 %copy-start.4 = (bf16[768,512]{1,0:T(8,128)(2,1)S(1)}, bf16[768,512]{1,0:T(8,128)(2,1)}, u32[]{:S(2)}) copy-start(bf16[768,512]{1,0:T(8,128)(2,1)} %reduce-scatter.2.cloned.1.call-done) | copy-start | bytes 2359300
Sparse Core Ops, SparseCore 0:
  10.5 135.6 all-gather.5
  148.0 69.2 all-gather.3
  220.8 200.1 all-gather.7
  436.0 68.2 reduce-scatter.1
where the time goes:
time: 531 us; the launch traced here: 530 us
  waiting for transfers between devices  376 us (71%)
  local copies, waits for them, and re-layouts  48.3 us (9%)
  matrix products  44.6 us (8%)
  blocking collectives  16 us (3%)
  between operations  13.9 us (3%)
  loops' own time  11.8 us (2%)
  starting transfers between devices  10.4 us (2%)
  other arithmetic  8.54 us (2%)
    all_gather x1, waiting for transfers between devices, on_device(): weight_rows = lax.all_gather(in_weight, 'ctx', axis=0, tiled=True)  163 us
    all_gather x1, waiting for transfers between devices, on_device(): gathered = lax.all_gather(grad_out, 'ch', axis=1, tiled=True)  71 us
    all_gather x1, waiting for transfers between devices, on_device(): lax.all_gather(out_weight, 'ctx', axis=1, tiled=True)  68.1 us
    reduce_scatter x1, waiting for transfers between devices, on_device(): lax.psum_scatter(hidden_terms.astype(jnp.bfloat16), 'ch', scatter_dimensi...  67.7 us
    rev x1, local copies, waits for them, and re-layouts, on_device(): flipped = table[:, ::-1, ::-1]  22.6 us
    psum x1, blocking collectives, on_device(): cross_sum = lax.psum(jnp.sum(scaled * source_in, axis=1), 'ch')  16 us
    dot_general x1, matrix products, on_device(): lax.dot_general(stacked, flat_rows, (((1,), (1,)), ((), ())), preferred_e...  14.8 us
    dot_general x6, matrix products, backward_tile(): jnp.einsum('gst,tgc->sgc', masked, source, preferred_element_type=jnp.flo...  13.6 us
  transfers between devices with their start and end apart: 8, of which 5 were waited for; matrix products, arithmetic and copies ran while one was open for 16% of the time, Pallas kernels for 0%

commit v1 on v0

v1 whole, which is shorter than its diff:
```python
import functools

import jax
import jax.numpy as jnp
from jax import lax
from jax.experimental import pallas as pl
from jax.experimental.pallas import tpu as pltpu
from jax.sharding import PartitionSpec as P

D = 4096
LEN = 128
GROUP = 16
DOCS = 4
EPS = 1e-05
TOK = 768
CH = 512
TILES = TOK // LEN
BLOCKS = CH // 128
STACK = 128 // GROUP
F32 = jnp.float32
BF16 = jnp.bfloat16
NT = (((1,), (1,)), ((), ()))


def aligned(index, size):
    return pl.ds(pl.multiple_of(index * size, size), size)


def loop(count, body, start=0):
    def step(index, carry):
        body(index)
        return carry

    lax.fori_loop(start, count, step, 0)


def kernel(
    go_h, x_h, gain_v, q_h, k_h, v_h, filt_v, docs_v, iw_h, ow_h, out_h,
    grads, wts, ows, xin, qry, key, val, prod, wg, mixed, acc, stk, tabf, tabb, base, mask,
    docs, parts, sibs, runs, sums, fin, outv,
    lsem, ags, agr, bs, br, p0s, p0r, ws, wr, hs, hr, us, ur, ss, sr, cs, cr,
):
    ctx = lax.axis_index("ctx")
    ch = lax.axis_index("ch")
    x = ctx % 4
    y = (ctx // 4) % 4
    z = ctx // 16
    k = ch // 2
    core = ch % 2
    sib = 2 * k + 1 - core
    started = []

    def local(src, dst, index):
        return pltpu.make_async_copy(src, dst, lsem.at[index])

    def remote(src, dst, send, recv, to_ctx, to_ch):
        return pltpu.make_async_remote_copy(
            src, dst, send, recv, device_id=(to_ctx, to_ch), device_id_type=pl.DeviceIdType.MESH
        )

    def go(copy, cond=None):
        if cond is None:
            copy.start()
        else:
            pl.when(cond)(copy.start)
        started.append((copy, cond))

    def when(cond, body):
        pl.when(cond)(body)

    loads = [
        local(k_h, key, 0),
        local(v_h, val, 1),
        local(iw_h, wts.at[:, z, y, x], 2),
        local(ow_h, ows.at[z, y, x], 3),
        local(go_h, grads.at[ch], 4),
        local(x_h, xin, 5),
        local(q_h, qry, 6),
    ]
    for load in loads:
        load.start()

    barrier = pltpu.get_barrier_semaphore()
    up = (ctx + 1) % 32
    down = (ctx + 31) % 32

    def plane(dy, dx):
        return z * 16 + ((y + dy) % 4) * 4 + (x + dx) % 4

    partner = (1 - z) * 16 + y * 4 + x
    greet = [plane(0, 1), plane(0, 3), plane(1, 0), plane(3, 0), partner, up, down]
    for peer in greet:
        pl.semaphore_signal(barrier, inc=1, device_id=(peer, ch), device_id_type=pl.DeviceIdType.MESH)
    for step in range(1, 8):
        pl.semaphore_signal(
            barrier, inc=1, device_id=(ctx, (ch + step) % 8), device_id_type=pl.DeviceIdType.MESH
        )
    pl.semaphore_wait(barrier, len(greet) + 7)

    def piece(w, zi, yi, xi, quarter):
        if w == 0:
            return ows.at[zi, yi, xi, pl.ds(quarter * 128, 128), :]
        return wts.at[:, zi, yi, xi, pl.ds(quarter * 32, 32), :]

    def ring_copy(w, zz, quarter, step):
        zi = z if zz == 0 else 1 - z
        shift = 3 if quarter % 2 == 0 else 1
        along_y = (quarter < 2) == (step < 3)
        hop = 1 if quarter % 2 == 0 else 3
        peer = plane(hop, 0) if along_y else plane(0, hop)
        if step < 3:
            back = shift * step
            yi = (y + back) % 4 if along_y else y
            xi = x if along_y else (x + back) % 4
            dst = piece(w, zi, yi, xi, quarter)
            src = dst
            if step == 0 and zz == 0:
                if w == 0:
                    src = ow_h.at[pl.ds(quarter * 128, 128), :]
                else:
                    src = iw_h.at[:, pl.ds(quarter * 32, 32), :]
        else:
            back = shift * (step - 3)
            if along_y:
                yi, xi = (y + back) % 4, slice(None)
            else:
                yi, xi = slice(None), (x + back) % 4
            dst = piece(w, zi, yi, xi, quarter)
            src = dst
        return remote(src, dst, ws.at[w, zz, quarter, step], wr.at[w, zz, quarter, step], peer, ch)

    def ring_arrival(w, zz, quarter, step):
        zi = z if zz == 0 else 1 - z
        shift = 3 if quarter % 2 == 0 else 1
        along_y = (quarter < 2) == (step < 3)
        back = shift * (step % 3 + 1)
        if step < 3:
            yi = (y + back) % 4 if along_y else y
            xi = x if along_y else (x + back) % 4
        elif along_y:
            yi, xi = (y + back) % 4, slice(None)
        else:
            yi, xi = slice(None), (x + back) % 4
        dst = piece(w, zi, yi, xi, quarter)
        return remote(dst, dst, ws.at[w, zz, quarter, step], wr.at[w, zz, quarter, step], ctx, ch)

    def swap_copy(w):
        if w == 0:
            return remote(ow_h, ows.at[z, y, x], p0s.at[0], p0r.at[0], partner, ch)
        return remote(iw_h, wts.at[:, z, y, x], p0s.at[1], p0r.at[1], partner, ch)

    def swap_arrival(w):
        dst = ows.at[1 - z, y, x] if w == 0 else wts.at[:, 1 - z, y, x]
        return remote(dst, dst, p0s.at[w], p0r.at[w], ctx, ch)

    def weights(w, zz, event):
        if event == 0 and zz == 1:
            swap_arrival(w).wait_recv()
        if event == 3 and zz == 0:
            loads[3 - w].wait()
        for quarter in range(4):
            if event >= 1:
                ring_arrival(w, zz, quarter, event - 1).wait_recv()
            if event <= 5:
                go(ring_copy(w, zz, quarter, event))

    def line_copy(src_k, side, step):
        d = 2 * src_k + core
        to = (ch + 2) % 8 if side == 0 else (ch + 6) % 8
        src = go_h if step == 0 else grads.at[d]
        return remote(src, grads.at[d], ags.at[side, step], agr.at[src_k], ctx, to)

    def sib_copy(src_k, step):
        d = 2 * src_k + core
        src = go_h if step == 0 else grads.at[d]
        return remote(src, grads.at[d], bs.at[src_k], br.at[src_k], ctx, sib)

    def line_relay(step):
        for side, src_k, have, more in (
            (0, k - step, k >= step, k < 3),
            (1, k + step, k + step <= 3, k > 0),
        ):
            def relay(side=side, src_k=src_k, more=more):
                d = 2 * src_k + core
                remote(grads.at[d], grads.at[d], ags.at[side, step], agr.at[src_k], ctx, ch).wait_recv()
                if step < 3:
                    pl.when(more)(line_copy(src_k, side, step).start)
                sib_copy(src_k, step).start()

            when(have, relay)

    def multiply(d):
        zi, yi = d // 4, d % 4
        wide = jnp.concatenate([ows[zi, yi, xi] for xi in range(4)], axis=1)

        def rows_of(m):
            rows = aligned(m, 256)
            acc[rows, :] = acc[rows, :] + lax.dot_general(
                grads[d, rows, :], wide, NT, preferred_element_type=F32
            )

        loop(3, rows_of)

    def line_multiply(step):
        def one(index):
            side, other = index // 2, index % 2
            src_k = k - step + 2 * step * side

            def act():
                def await_sibling():
                    d = 2 * src_k + 1 - core
                    remote(grads.at[d], grads.at[d], bs.at[src_k], br.at[src_k], ctx, ch).wait_recv()

                when(other == 1, await_sibling)
                multiply(2 * src_k + core + other * (1 - 2 * core))

            when((src_k >= 0) & (src_k <= 3), act)

        loop(4, one)

    go(swap_copy(0))
    weights(0, 0, 0)
    go(line_copy(k, 0, 0), k < 3)
    go(line_copy(k, 1, 0), k > 0)
    go(sib_copy(k, 0))
    weights(1, 0, 0)
    go(swap_copy(1))
    wide_row = lax.broadcasted_iota(jnp.int32, (8, 2 * LEN), 0)
    own = jnp.zeros((8, 2 * LEN), jnp.int32)
    for i in range(DOCS):
        own = jnp.where(wide_row == i, docs_v[0:1, i : i + 1], own)
    docs[0] = own
    go(remote(docs.at[0], docs.at[1], hs.at[0], hr.at[0], up, ch))
    go(remote(docs.at[0], docs.at[2], hs.at[1], hr.at[1], down, ch))

    loads[0].wait()
    loads[1].wait()

    def product(i):
        rows = aligned(i, LEN)
        prod[pl.ds(pl.multiple_of(i * LEN + LEN, LEN), LEN), :] = (
            key[rows, :].astype(F32) * val[rows, :].astype(F32)
        ).astype(BF16)

    loop(TILES, product)
    go(remote(prod.at[pl.ds(TOK, LEN), :], prod.at[pl.ds(0, LEN), :], hs.at[2], hr.at[2], up, ch))
    weights(0, 0, 1)

    taps = filt_v[...]
    flip_row = lax.broadcasted_iota(jnp.int32, (LEN, 2 * LEN), 0)
    flip_col = lax.broadcasted_iota(jnp.int32, (LEN, 2 * LEN), 1)
    flip = jnp.where(flip_row + flip_col == LEN, 1.0, 0.0).astype(BF16)
    base[0] = jnp.dot(taps, flip, preferred_element_type=F32)
    base[1] = jnp.concatenate([taps.astype(F32), jnp.zeros((32, LEN), F32)], axis=1)

    def build(which, tab):
        def one(g):
            row = jnp.broadcast_to(base[which, pl.ds(g, 1), :], (LEN, 2 * LEN))
            tab[g] = pltpu.roll(row, 0, 1, stride=1, stride_axis=0).astype(BF16)

        loop(BLOCKS * STACK, one)

    build(0, tabf)
    weights(0, 1, 0)
    weights(1, 0, 1)

    loads[5].wait()

    def row_sums(i, which, wide):
        narrow = wide[:, 0:128] + wide[:, 128:256] + wide[:, 256:384] + wide[:, 384:512]
        sums[which, ch, pl.ds(i, 1), :] = jnp.sum(narrow.T, axis=0, keepdims=True)

    sums[0, ch] = jnp.zeros((8, 128), F32)
    sums[1, ch] = jnp.zeros((8, 128), F32)

    def squares(i):
        block = xin[aligned(i, LEN), :].astype(F32)
        row_sums(i, 0, block * block)

    loop(TILES, squares)

    def send_sums(which):
        for step in range(1, 8):
            to = (ch + step) % 8
            go(remote(sums.at[which, ch], sums.at[which, ch], us.at[which, step], ur.at[which, step], ctx, to))

    def await_sums(which):
        for step in range(1, 8):
            src = (ch + 8 - step) % 8
            remote(
                sums.at[which, src], sums.at[which, src], us.at[which, step], ur.at[which, step], ctx, ch
            ).wait_recv()

    send_sums(0)
    weights(0, 0, 2)
    weights(0, 1, 1)
    weights(1, 0, 2)
    build(1, tabb)
    weights(0, 0, 3)
    weights(0, 1, 2)
    weights(1, 0, 3)

    lane_group = lax.broadcasted_iota(jnp.int32, (LEN, 128), 1) // GROUP
    row_pos = lax.broadcasted_iota(jnp.int32, (LEN, 2 * LEN), 0)
    col_pos = lax.broadcasted_iota(jnp.int32, (LEN, 2 * LEN), 1)

    def set_mask(source, target, starts):
        cut = jnp.zeros((LEN, 2 * LEN), F32)
        for first in starts:
            cut = jnp.where((source < first) & (first <= target), 1.0, cut)
        mask[...] = (1.0 - cut).astype(BF16)

    def convolve(tab, src, i, b):
        lanes = aligned(b, 128)
        block = src[pl.ds(pl.multiple_of(i * LEN, LEN), 2 * LEN), lanes]
        left = (tab[pl.ds(pl.multiple_of(b * STACK, STACK), STACK)] * mask[...][None]).reshape(
            STACK * LEN, 2 * LEN
        )
        every = jnp.dot(left, block, preferred_element_type=F32).reshape(STACK, LEN, 128)
        picked = every[0]
        for g in range(1, STACK):
            picked = jnp.where(lane_group == g, every[g], picked)
        return picked

    def forward(i):
        set_mask(
            col_pos + (i * LEN - LEN),
            row_pos + i * LEN,
            [docs[0, r : r + 1, :] for r in range(DOCS)] + [docs[1, DOCS - 1 : DOCS, :] - TOK],
        )

        def one(b):
            mixed[aligned(i, LEN), aligned(b, 128)] = convolve(tabf, prod, i, b)

        loop(BLOCKS, one)

    remote(docs.at[0], docs.at[1], hs.at[0], hr.at[0], ctx, ch).wait_recv()
    loop(3, forward, 1)
    weights(0, 1, 3)
    weights(0, 0, 4)
    weights(1, 1, 0)
    loop(TILES, forward, 3)
    weights(0, 0, 5)
    weights(0, 1, 4)
    remote(prod.at[pl.ds(TOK, LEN), :], prod.at[pl.ds(0, LEN), :], hs.at[2], hr.at[2], ctx, ch).wait_recv()
    loop(1, forward)
    line_relay(1)
    weights(1, 0, 4)
    weights(0, 0, 6)
    weights(0, 1, 5)
    weights(0, 1, 6)
    weights(1, 1, 1)

    loads[4].wait()
    acc[...] = jnp.zeros((TOK, CH), F32)
    multiply(2 * k + core)
    remote(grads.at[sib], grads.at[sib], bs.at[k], br.at[k], ctx, ch).wait_recv()
    multiply(sib)
    line_multiply(1)
    weights(1, 0, 5)
    weights(1, 1, 2)
    line_relay(2)
    line_multiply(2)
    weights(1, 1, 3)
    weights(1, 0, 6)
    line_relay(3)
    line_multiply(3)
    weights(1, 1, 4)

    loads[6].wait()

    def gates(i):
        rows = aligned(i, LEN)
        mix = acc[rows, :]
        wg[rows, :] = (mix * qry[rows, :].astype(F32)).astype(BF16)
        stk[0, rows, :] = (mix * mixed[rows, :]).astype(BF16)

    loop(1, gates)
    go(remote(wg.at[pl.ds(0, LEN), :], wg.at[pl.ds(TOK, LEN), :], hs.at[3], hr.at[3], down, ch))
    loop(TILES, gates, 1)
    remote(docs.at[0], docs.at[2], hs.at[1], hr.at[1], ctx, ch).wait_recv()

    def backward(i):
        set_mask(
            row_pos + i * LEN,
            col_pos + i * LEN,
            [docs[0, r : r + 1, :] for r in range(DOCS)]
            + [docs[2, r : r + 1, :] + TOK for r in range(DOCS)],
        )

        def one(b):
            rows, lanes = aligned(i, LEN), aligned(b, 128)
            conv = convolve(tabb, wg, i, b)
            stk[1, rows, lanes] = (conv * val[rows, lanes].astype(F32)).astype(BF16)
            stk[2, rows, lanes] = (conv * key[rows, lanes].astype(F32)).astype(BF16)

        loop(BLOCKS, one)

    loop(TILES - 1, backward)
    weights(1, 1, 5)
    remote(wg.at[pl.ds(0, LEN), :], wg.at[pl.ds(TOK, LEN), :], hs.at[3], hr.at[3], ctx, ch).wait_recv()
    loop(TILES, backward, TILES - 1)
    weights(1, 1, 6)

    order = [3 * (1 - k // 2), (2 + 3 * k) % 5, 1 + k % 2, k]

    def partials(j):
        def one(part):
            d = 2 * j + (1 - core) * (1 - part) + core * part
            zi, yi = d // 4, d % 4

            def rows_of(m):
                rows = aligned(m, 256)
                total = lax.dot_general(
                    stk[0, rows, :], wts[0, zi, yi].reshape(CH, CH), NT, preferred_element_type=F32
                )
                for b in (1, 2):
                    total = total + lax.dot_general(
                        stk[b, rows, :], wts[b, zi, yi].reshape(CH, CH), NT, preferred_element_type=F32
                    )
                parts[part, j, rows, :] = total.astype(BF16)

            loop(3, rows_of)

            def send():
                remote(parts.at[0, j], sibs.at[j], ss.at[j], sr.at[j], ctx, sib).start()

            when(part == 0, send)

        loop(2, one)

    def await_sib(j):
        remote(parts.at[0, j], sibs.at[j], ss.at[j], sr.at[j], ctx, ch).wait_recv()

    def run_arrival(slot):
        remote(runs.at[slot], runs.at[slot], cs.at[0], cr.at[slot], ctx, ch).wait_recv()

    def chain_copy(j, side):
        to = (ch + 2) % 8 if side == 0 else (ch + 6) % 8
        slot = j + 4 * side
        return remote(parts.at[1, j], runs.at[slot], cs.at[j], cr.at[slot], ctx, to)

    def forward_sum(j):
        await_sib(j)
        inner = (k == 1) | (k == 2)
        slot = j + 4 * ((k - j + 3) // 4)

        def with_run():
            run_arrival(slot)

            def add(i):
                rows = aligned(i, LEN)
                parts[1, j, rows, :] = (
                    parts[1, j, rows, :].astype(F32)
                    + sibs[j, rows, :].astype(F32)
                    + runs[slot, rows, :].astype(F32)
                ).astype(BF16)

            loop(TILES, add)

        def without_run():
            def add(i):
                rows = aligned(i, LEN)
                parts[1, j, rows, :] = (
                    parts[1, j, rows, :].astype(F32) + sibs[j, rows, :].astype(F32)
                ).astype(BF16)

            loop(TILES, add)

        when(inner, with_run)
        when(jnp.logical_not(inner), without_run)
        when(j > k, chain_copy(j, 0).start)
        when(j < k, chain_copy(j, 1).start)

    def clear(slot):
        def one():
            runs[slot] = jnp.zeros((TOK, CH), BF16)

        return one

    when(k == 0, clear(0))
    when(k == 3, clear(7))
    partials(order[0])
    partials(order[1])
    forward_sum(order[0])
    forward_sum(order[1])
    partials(order[2])
    forward_sum(order[2])
    partials(order[3])
    await_sib(k)
    when(k > 0, lambda: run_arrival(k))
    when(k < 3, lambda: run_arrival(4 + k))

    gain = gain_v[...].astype(F32)

    def cross(i):
        rows = aligned(i, LEN)
        norm = (
            parts[1, k, rows, :].astype(F32)
            + sibs[k, rows, :].astype(F32)
            + runs[k, rows, :].astype(F32)
            + runs[4 + k, rows, :].astype(F32)
        )
        scaled = gain * norm
        acc[rows, :] = scaled
        row_sums(i, 1, scaled * xin[rows, :].astype(F32))

    loop(TILES, cross)
    send_sums(1)
    await_sums(0)
    await_sums(1)

    def total(which):
        full = sums[which, 0]
        for src in range(1, 8):
            full = full + sums[which, src]
        return full

    fin[0] = lax.rsqrt(total(0) / D + EPS)
    fin[1] = total(1) / D

    def column(row):
        tall = jnp.broadcast_to(row, (128, 128)).T
        return jnp.concatenate([tall] * BLOCKS, axis=1)

    def finish(i):
        rows = aligned(i, LEN)
        inverse = column(fin[0, pl.ds(i, 1), :])
        crossed = column(fin[1, pl.ds(i, 1), :])
        outv[rows, :] = (
            grads[ch, rows, :].astype(F32)
            + inverse * acc[rows, :]
            - xin[rows, :].astype(F32) * (inverse * inverse * inverse) * crossed
        ).astype(BF16)

    loop(TILES, finish)
    store = local(outv, out_h, 7)
    store.start()

    for copy, cond in started:
        if cond is None:
            copy.wait_send()
        else:
            pl.when(cond)(copy.wait_send)
    for step in (1, 2, 3):
        for side, src_k, have, more in (
            (0, k - step, k >= step, k < 3),
            (1, k + step, k + step <= 3, k > 0),
        ):
            def drain(side=side, src_k=src_k, more=more):
                if step < 3:
                    pl.when(more)(line_copy(src_k, side, step).wait_send)
                sib_copy(src_k, step).wait_send()

            when(have, drain)
    for j in order:
        remote(parts.at[0, j], sibs.at[j], ss.at[j], sr.at[j], ctx, sib).wait_send()
        when(j > k, chain_copy(j, 0).wait_send)
        when(j < k, chain_copy(j, 1).wait_send)
    store.wait()


def on_device(
    grad_out, block_input, norm_gain, queries, keys, values, filters, doc_starts, in_weight, out_weight
):
    hbm = pl.BlockSpec(memory_space=pl.ANY)
    vmem = pl.BlockSpec(memory_space=pltpu.VMEM)
    dma = pltpu.SemaphoreType.DMA
    return pl.pallas_call(
        kernel,
        out_shape=jax.ShapeDtypeStruct((TOK, CH), BF16),
        in_specs=[hbm, hbm, vmem, hbm, hbm, hbm, vmem, vmem, hbm, hbm],
        out_specs=hbm,
        scratch_shapes=[
            pltpu.VMEM((8, TOK, CH), BF16),
            pltpu.VMEM((3, 2, 4, 4, 128, CH), BF16),
            pltpu.VMEM((2, 4, 4, CH, 128), BF16),
            pltpu.VMEM((TOK, CH), BF16),
            pltpu.VMEM((TOK, CH), BF16),
            pltpu.VMEM((TOK, CH), BF16),
            pltpu.VMEM((TOK, CH), BF16),
            pltpu.VMEM((TOK + LEN, CH), BF16),
            pltpu.VMEM((TOK + LEN, CH), BF16),
            pltpu.VMEM((TOK, CH), F32),
            pltpu.VMEM((TOK, CH), F32),
            pltpu.VMEM((3, TOK, CH), BF16),
            pltpu.VMEM((32, LEN, 2 * LEN), BF16),
            pltpu.VMEM((32, LEN, 2 * LEN), BF16),
            pltpu.VMEM((2, 32, 2 * LEN), F32),
            pltpu.VMEM((LEN, 2 * LEN), BF16),
            pltpu.VMEM((3, 8, 2 * LEN), jnp.int32),
            pltpu.VMEM((2, 4, TOK, CH), BF16),
            pltpu.VMEM((4, TOK, CH), BF16),
            pltpu.VMEM((8, TOK, CH), BF16),
            pltpu.VMEM((2, 8, 8, 128), F32),
            pltpu.VMEM((2, 8, 128), F32),
            pltpu.VMEM((TOK, CH), BF16),
            dma((8,)),
            dma((2, 3)),
            dma((4,)),
            dma((4,)),
            dma((4,)),
            dma((2,)),
            dma((2,)),
            dma((2, 2, 4, 6)),
            dma((2, 2, 4, 6)),
            dma((4,)),
            dma((4,)),
            dma((2, 8)),
            dma((2, 8)),
            dma((4,)),
            dma((4,)),
            dma((4,)),
            dma((8,)),
        ],
        compiler_params=pltpu.CompilerParams(
            collective_id=0, has_side_effects=True, vmem_limit_bytes=66 * 1024 * 1000
        ),
    )(
        grad_out,
        block_input,
        norm_gain.reshape(1, -1),
        queries,
        keys,
        values,
        filters,
        doc_starts,
        jnp.transpose(in_weight, (1, 0, 2)),
        out_weight,
    )


def solution(mesh):
    placed = (
        P("ctx", "ch"),
        P("ctx", "ch"),
        P("ch"),
        P("ctx", "ch"),
        P("ctx", "ch"),
        P("ctx", "ch"),
        P("ch", None),
        P("ctx", None),
        P("ctx", None, "ch"),
        P("ch", "ctx"),
    )
    return jax.shard_map(
        on_device, mesh=mesh, in_specs=placed, out_specs=P("ctx", "ch"), check_vma=False
    )
```

time: 531 us -> 214 us (0.40)
  waiting for transfers between devices: 376 us -> 0 us
  Pallas kernels: 0 us -> 211 us
  local copies, waits for them, and re-layouts: 48.3 us -> 3.32 us
  matrix products: 44.6 us -> 0 us
  blocking collectives: 16 us -> 0 us
  between operations: 13.9 us -> 0.01 us
  loops' own time: 11.8 us -> 0 us
  starting transfers between devices: 10.4 us -> 0 us
  other arithmetic: 8.54 us -> 0 us
    all_gather x3 -> x0, waiting for transfers between devices: 302 us -> none  [the longest x1 163 us: on_device(): weight_rows = lax.all_gather(in_weight, 'ctx', axis=0, tiled=True)]
    pallas_call x0 -> x1, Pallas kernels: none -> 211 us  [on_device(): pl.pallas_call(kernel, out_shape=jax.ShapeDtypeStruct((TOK, CH), BF16), i...]
    reduce_scatter x1 -> x0, waiting for transfers between devices: 67.7 us -> none  [on_device(): lax.psum_scatter(hidden_terms.astype(jnp.bfloat16), 'ch', scatter_dimensi...]
    dot_general x15 -> x0, matrix products: 44.6 us -> none  [the longest x1 14.8 us: on_device(): lax.dot_general(stacked, flat_rows, (((1,), (1,)), ((), ())), preferred_e...]
    rev x1 -> x0, local copies, waits for them, and re-layouts: 22.6 us -> none  [on_device(): flipped = table[:, ::-1, ::-1]]
    psum x1 -> x0, blocking collectives: 16 us -> none  [on_device(): cross_sum = lax.psum(jnp.sum(scaled * source_in, axis=1), 'ch')]
    dynamic_slice x48 -> x0, local copies, waits for them, and re-layouts: 15.6 us -> none  [the longest x12 7.12 us: on_device(): lax.map(forward_tile, jnp.arange(tile_count, dtype=jnp.int32))]
    another operation x2 -> x0, loops' own time: 11.8 us -> none  [the longest x1 8 us: on_device(): lax.map(forward_tile, jnp.arange(tile_count, dtype=jnp.int32))]
  transfers between devices with their start and end apart: 8 -> 0, of which waited for: 5 -> 0; matrix products, arithmetic and copies ran while one was open for 16% -> 0% of each run, Pallas kernels for 0% -> 0%
where the time goes in v1:
time: 214 us
  Pallas kernels  211 us (99%)
  local copies, waits for them, and re-layouts  3.32 us (2%)
    pallas_call x1, Pallas kernels, on_device(): pl.pallas_call(kernel, out_shape=jax.ShapeDtypeStruct((TOK, CH), BF16), i...  211 us

profile of v1, /device:TPU:1, one launch (start us, length us, event | category | flops | bytes accessed | tf_op | source)
XLA Modules:
  0.0 213.9 jit_solution(4265997662008744020)
XLA Ops:
  0.0 0.0 copy-start
  0.0 0.7 copy-done
  0.7 0.6 reshape.3.gain_v
  1.3 210.6 %shard_map.100 = bf16[768,512]{1,0:T(8,128)(2,1)} custom-call(bf16[768,512]{1,0:T(8,128)(2,1)} %go_h.1, bf16[768,512]{1,0:T(8,128)(2,1)} %x_h.1, bf16[1,512]{1,0:T(2,128)(2,1)} %reshape.3.gain_v, bf16[768,512]{1,0:T(8,128)(2,1)} %q_h.1, bf16[768,512]{1,0:T(8,128)(2,1)} %k_h.1, bf16[768,512]{1,0:T(8,128)(2,1)} %v_h.1, bf16[32,128]{1,0:T(8,128)(2,1)} %filt_v.1, ...), custom_call_target="tpu_custom_call" | custom-call | tf_op jit(solution)/shard_map/pallas_call | solution.py:569
  211.8 2.1 copy.12
Async XLA Ops:
  0.0 0.7 copy-start

commit v2 on v1

--- a/solution.py
+++ b/solution.py
@@ -23,7 +23,7 @@
 
 
 def aligned(index, size):
-    return pl.ds(pl.multiple_of(index * size, size), size)
+    return pl.ds(index * size if isinstance(index, int) else pl.multiple_of(index * size, size), size)
 
 
 def loop(count, body, start=0):
@@ -95,6 +95,54 @@
         pl.semaphore_signal(
             barrier, inc=1, device_id=(ctx, (ch + step) % 8), device_id_type=pl.DeviceIdType.MESH
         )
+    wide_row = lax.broadcasted_iota(jnp.int32, (8, 2 * LEN), 0)
+    own = jnp.zeros((8, 2 * LEN), jnp.int32)
+    for i in range(DOCS):
+        own = jnp.where(wide_row == i, docs_v[0:1, i : i + 1], own)
+    docs[0] = own
+
+    loads[0].wait()
+    loads[1].wait()
+
+    def product(i):
+        rows = aligned(i, LEN)
+        prod[pl.ds(pl.multiple_of(i * LEN + LEN, LEN), LEN), :] = (
+            key[rows, :].astype(F32) * val[rows, :].astype(F32)
+        ).astype(BF16)
+
+    loop(TILES, product)
+
+    taps = filt_v[...]
+    flip_row = lax.broadcasted_iota(jnp.int32, (LEN, 2 * LEN), 0)
+    flip_col = lax.broadcasted_iota(jnp.int32, (LEN, 2 * LEN), 1)
+    flip = jnp.where(flip_row + flip_col == LEN, 1.0, 0.0).astype(BF16)
+    base[0] = jnp.dot(taps, flip, preferred_element_type=F32)
+    base[1] = jnp.concatenate([taps.astype(F32), jnp.zeros((32, LEN), F32)], axis=1)
+
+    def build(which, tab):
+        def one(g):
+            row = jnp.broadcast_to(base[which, pl.ds(g, 1), :], (LEN, 2 * LEN))
+            tab[g] = pltpu.roll(row, 0, 1, stride=1, stride_axis=0).astype(BF16)
+
+        loop(BLOCKS * STACK, one)
+
+    build(0, tabf)
+
+    loads[5].wait()
+
+    def row_sums(i, which, wide):
+        narrow = wide[:, 0:128] + wide[:, 128:256] + wide[:, 256:384] + wide[:, 384:512]
+        sums[which, ch, pl.ds(i, 1), :] = jnp.sum(narrow.T, axis=0, keepdims=True)
+
+    sums[0, ch] = jnp.zeros((8, 128), F32)
+    sums[1, ch] = jnp.zeros((8, 128), F32)
+
+    def squares(i):
+        block = xin[aligned(i, LEN), :].astype(F32)
+        row_sums(i, 0, block * block)
+
+    loop(TILES, squares)
+
     pl.semaphore_wait(barrier, len(greet) + 7)
 
     def piece(w, zi, yi, xi, quarter):
@@ -218,66 +266,16 @@
 
         loop(4, one)
 
+    go(remote(docs.at[0], docs.at[1], hs.at[0], hr.at[0], up, ch))
+    go(remote(docs.at[0], docs.at[2], hs.at[1], hr.at[1], down, ch))
+    weights(0, 0, 0)
+    weights(1, 0, 0)
+    go(remote(prod.at[pl.ds(TOK, LEN), :], prod.at[pl.ds(0, LEN), :], hs.at[2], hr.at[2], up, ch))
     go(swap_copy(0))
-    weights(0, 0, 0)
+    go(swap_copy(1))
     go(line_copy(k, 0, 0), k < 3)
     go(line_copy(k, 1, 0), k > 0)
     go(sib_copy(k, 0))
-    weights(1, 0, 0)
-    go(swap_copy(1))
-    wide_row = lax.broadcasted_iota(jnp.int32, (8, 2 * LEN), 0)
-    own = jnp.zeros((8, 2 * LEN), jnp.int32)
-    for i in range(DOCS):
-        own = jnp.where(wide_row == i, docs_v[0:1, i : i + 1], own)
-    docs[0] = own
-    go(remote(docs.at[0], docs.at[1], hs.at[0], hr.at[0], up, ch))
-    go(remote(docs.at[0], docs.at[2], hs.at[1], hr.at[1], down, ch))
-
-    loads[0].wait()
-    loads[1].wait()
-
-    def product(i):
-        rows = aligned(i, LEN)
-        prod[pl.ds(pl.multiple_of(i * LEN + LEN, LEN), LEN), :] = (
-            key[rows, :].astype(F32) * val[rows, :].astype(F32)
-        ).astype(BF16)
-
-    loop(TILES, product)
-    go(remote(prod.at[pl.ds(TOK, LEN), :], prod.at[pl.ds(0, LEN), :], hs.at[2], hr.at[2], up, ch))
-    weights(0, 0, 1)
-
-    taps = filt_v[...]
-    flip_row = lax.broadcasted_iota(jnp.int32, (LEN, 2 * LEN), 0)
-    flip_col = lax.broadcasted_iota(jnp.int32, (LEN, 2 * LEN), 1)
-    flip = jnp.where(flip_row + flip_col == LEN, 1.0, 0.0).astype(BF16)
-    base[0] = jnp.dot(taps, flip, preferred_element_type=F32)
-    base[1] = jnp.concatenate([taps.astype(F32), jnp.zeros((32, LEN), F32)], axis=1)
-
-    def build(which, tab):
-        def one(g):
-            row = jnp.broadcast_to(base[which, pl.ds(g, 1), :], (LEN, 2 * LEN))
-            tab[g] = pltpu.roll(row, 0, 1, stride=1, stride_axis=0).astype(BF16)
-
-        loop(BLOCKS * STACK, one)
-
-    build(0, tabf)
-    weights(0, 1, 0)
-    weights(1, 0, 1)
-
-    loads[5].wait()
-
-    def row_sums(i, which, wide):
-        narrow = wide[:, 0:128] + wide[:, 128:256] + wide[:, 256:384] + wide[:, 384:512]
-        sums[which, ch, pl.ds(i, 1), :] = jnp.sum(narrow.T, axis=0, keepdims=True)
-
-    sums[0, ch] = jnp.zeros((8, 128), F32)
-    sums[1, ch] = jnp.zeros((8, 128), F32)
-
-    def squares(i):
-        block = xin[aligned(i, LEN), :].astype(F32)
-        row_sums(i, 0, block * block)
-
-    loop(TILES, squares)
 
     def send_sums(which):
         for step in range(1, 8):
@@ -292,13 +290,6 @@
             ).wait_recv()
 
     send_sums(0)
-    weights(0, 0, 2)
-    weights(0, 1, 1)
-    weights(1, 0, 2)
-    build(1, tabb)
-    weights(0, 0, 3)
-    weights(0, 1, 2)
-    weights(1, 0, 3)
 
     lane_group = lax.broadcasted_iota(jnp.int32, (LEN, 128), 1) // GROUP
     row_pos = lax.broadcasted_iota(jnp.int32, (LEN, 2 * LEN), 0)
@@ -312,7 +303,8 @@
 
     def convolve(tab, src, i, b):
         lanes = aligned(b, 128)
-        block = src[pl.ds(pl.multiple_of(i * LEN, LEN), 2 * LEN), lanes]
+        first = i * LEN if isinstance(i, int) else pl.multiple_of(i * LEN, LEN)
+        block = src[pl.ds(first, 2 * LEN), lanes]
         left = (tab[pl.ds(pl.multiple_of(b * STACK, STACK), STACK)] * mask[...][None]).reshape(
             STACK * LEN, 2 * LEN
         )
@@ -323,49 +315,54 @@
         return picked
 
     def forward(i):
-        set_mask(
-            col_pos + (i * LEN - LEN),
-            row_pos + i * LEN,
-            [docs[0, r : r + 1, :] for r in range(DOCS)] + [docs[1, DOCS - 1 : DOCS, :] - TOK],
-        )
+        firsts = [docs[0, r : r + 1, :] for r in range(DOCS)]
+        if isinstance(i, int):
+            firsts.append(docs[1, DOCS - 1 : DOCS, :] - TOK)
+        set_mask(col_pos + (i * LEN - LEN), row_pos + i * LEN, firsts)
 
         def one(b):
             mixed[aligned(i, LEN), aligned(b, 128)] = convolve(tabf, prod, i, b)
 
         loop(BLOCKS, one)
 
+    for event in (1, 2, 3):
+        weights(0, 0, event)
+        weights(1, 0, event)
+    loop(TILES, forward, 3)
+    weights(0, 1, 0)
+    weights(0, 0, 4)
+    weights(0, 1, 1)
+    weights(1, 0, 4)
+    weights(1, 1, 0)
+    weights(0, 0, 5)
+    weights(0, 1, 2)
+    line_relay(1)
+    weights(1, 1, 1)
+    weights(0, 1, 3)
+    weights(1, 1, 2)
+    weights(0, 1, 4)
+    build(1, tabb)
+    weights(1, 1, 3)
+    loop(3, forward, 1)
+    remote(prod.at[pl.ds(TOK, LEN), :], prod.at[pl.ds(0, LEN), :], hs.at[2], hr.at[2], ctx, ch).wait_recv()
     remote(docs.at[0], docs.at[1], hs.at[0], hr.at[0], ctx, ch).wait_recv()
-    loop(3, forward, 1)
-    weights(0, 1, 3)
-    weights(0, 0, 4)
-    weights(1, 1, 0)
-    loop(TILES, forward, 3)
-    weights(0, 0, 5)
-    weights(0, 1, 4)
-    remote(prod.at[pl.ds(TOK, LEN), :], prod.at[pl.ds(0, LEN), :], hs.at[2], hr.at[2], ctx, ch).wait_recv()
-    loop(1, forward)
-    line_relay(1)
-    weights(1, 0, 4)
+    forward(0)
+    line_relay(2)
+    weights(0, 1, 5)
+    weights(1, 1, 4)
+    weights(0, 1, 6)
     weights(0, 0, 6)
-    weights(0, 1, 5)
-    weights(0, 1, 6)
-    weights(1, 1, 1)
-
     loads[4].wait()
     acc[...] = jnp.zeros((TOK, CH), F32)
     multiply(2 * k + core)
     remote(grads.at[sib], grads.at[sib], bs.at[k], br.at[k], ctx, ch).wait_recv()
     multiply(sib)
+    weights(1, 0, 5)
     line_multiply(1)
-    weights(1, 0, 5)
-    weights(1, 1, 2)
-    line_relay(2)
+    line_relay(3)
     line_multiply(2)
-    weights(1, 1, 3)
-    weights(1, 0, 6)
-    line_relay(3)
+    weights(1, 1, 5)
     line_multiply(3)
-    weights(1, 1, 4)
 
     loads[6].wait()
 
@@ -397,80 +394,85 @@
         loop(BLOCKS, one)
 
     loop(TILES - 1, backward)
-    weights(1, 1, 5)
+    weights(1, 0, 6)
     remote(wg.at[pl.ds(0, LEN), :], wg.at[pl.ds(TOK, LEN), :], hs.at[3], hr.at[3], ctx, ch).wait_recv()
     loop(TILES, backward, TILES - 1)
     weights(1, 1, 6)
 
     order = [3 * (1 - k // 2), (2 + 3 * k) % 5, 1 + k % 2, k]
 
-    def partials(j):
+    def target(pos):
+        return sum(order[i] * ((4 - (pos + 4 - i) % 4) // 4) for i in range(4))
+
+    def chunk(c):
+        return aligned(c, 256)
+
+    def sib_part(j, c, to):
+        rows = chunk(c)
+        return remote(parts.at[0, j, rows], sibs.at[j, rows], ss.at[j, c], sr.at[j, c], ctx, to)
+
+    def run_arrival(slot, c):
+        rows = chunk(c)
+        remote(runs.at[slot, rows], runs.at[slot, rows], cs.at[0, c], cr.at[slot, c], ctx, ch).wait_recv()
+
+    def chain_copy(j, c, side):
+        rows = chunk(c)
+        to = (ch + 2) % 8 if side == 0 else (ch + 6) % 8
+        slot = j + 4 * side
+        return remote(parts.at[1, j, rows], runs.at[slot, rows], cs.at[j, c], cr.at[slot, c], ctx, to)
+
+    def partials(j, c):
+        rows = chunk(c)
+
         def one(part):
             d = 2 * j + (1 - core) * (1 - part) + core * part
             zi, yi = d // 4, d % 4
-
-            def rows_of(m):
-                rows = aligned(m, 256)
-                total = lax.dot_general(
-                    stk[0, rows, :], wts[0, zi, yi].reshape(CH, CH), NT, preferred_element_type=F32
+            total = lax.dot_general(
+                stk[0, rows, :], wts[0, zi, yi].reshape(CH, CH), NT, preferred_element_type=F32
+            )
+            for b in (1, 2):
+                total = total + lax.dot_general(
+                    stk[b, rows, :], wts[b, zi, yi].reshape(CH, CH), NT, preferred_element_type=F32
                 )
-                for b in (1, 2):
-                    total = total + lax.dot_general(
-                        stk[b, rows, :], wts[b, zi, yi].reshape(CH, CH), NT, preferred_element_type=F32
-                    )
-                parts[part, j, rows, :] = total.astype(BF16)
-
-            loop(3, rows_of)
-
-            def send():
-                remote(parts.at[0, j], sibs.at[j], ss.at[j], sr.at[j], ctx, sib).start()
-
-            when(part == 0, send)
+            parts[part, j, rows, :] = total.astype(BF16)
+            when(part == 0, sib_part(j, c, sib).start)
 
         loop(2, one)
 
-    def await_sib(j):
-        remote(parts.at[0, j], sibs.at[j], ss.at[j], sr.at[j], ctx, ch).wait_recv()
-
-    def run_arrival(slot):
-        remote(runs.at[slot], runs.at[slot], cs.at[0], cr.at[slot], ctx, ch).wait_recv()
-
-    def chain_copy(j, side):
-        to = (ch + 2) % 8 if side == 0 else (ch + 6) % 8
-        slot = j + 4 * side
-        return remote(parts.at[1, j], runs.at[slot], cs.at[j], cr.at[slot], ctx, to)
-
-    def forward_sum(j):
-        await_sib(j)
+    def forward_sum(j, c):
+        sib_part(j, c, ch).wait_recv()
         inner = (k == 1) | (k == 2)
         slot = j + 4 * ((k - j + 3) // 4)
 
+        def pieces(i):
+            return pl.ds(pl.multiple_of(c * 256 + i * 64, 64), 64)
+
         def with_run():
-            run_arrival(slot)
+            run_arrival(slot, c)
 
             def add(i):
-                rows = aligned(i, LEN)
+                rows = pieces(i)
                 parts[1, j, rows, :] = (
                     parts[1, j, rows, :].astype(F32)
                     + sibs[j, rows, :].astype(F32)
                     + runs[slot, rows, :].astype(F32)
                 ).astype(BF16)
 
-            loop(TILES, add)
+            loop(4, add)
 
         def without_run():
             def add(i):
-                rows = aligned(i, LEN)
+                rows = pieces(i)
                 parts[1, j, rows, :] = (
                     parts[1, j, rows, :].astype(F32) + sibs[j, rows, :].astype(F32)
                 ).astype(BF16)
 
-            loop(TILES, add)
+            loop(4, add)
 
         when(inner, with_run)
         when(jnp.logical_not(inner), without_run)
-        when(j > k, chain_copy(j, 0).start)
-        when(j < k, chain_copy(j, 1).start)
+        when(j > k, chain_copy(j, c, 0).start)
+        when(j < k, chain_copy(j, c, 1).start)
 
     def clear(slot):
         def one():
@@ -480,17 +482,30 @@
 
     when(k == 0, clear(0))
     when(k == 3, clear(7))
-    partials(order[0])
-    partials(order[1])
-    forward_sum(order[0])
-    forward_sum(order[1])
-    partials(order[2])
-    forward_sum(order[2])
-    partials(order[3])
-    await_sib(k)
-    when(k > 0, lambda: run_arrival(k))
-    when(k < 3, lambda: run_arrival(4 + k))
-
+
+    def job(n):
+        partials(target(n // 3), n % 3)
+        done = n - 2
+
+        def behind():
+            forward_sum(target(done // 3), done % 3)
+
+        when((done >= 0) & (done < 9), behind)
+
+    loop(12, job)
+
+    def total(which):
+        full = sums[which, 0]
+        for src in range(1, 8):
+            full = full + sums[which, src]
+        return full
+
+    def column(row):
+        tall = jnp.broadcast_to(row, (128, 128)).T
+        return jnp.concatenate([tall] * BLOCKS, axis=1)
+
+    await_sums(0)
+    fin[0] = lax.rsqrt(total(0) / D + EPS)
     gain = gain_v[...].astype(F32)
 
     def cross(i):
@@ -505,33 +520,26 @@
         acc[rows, :] = scaled
         row_sums(i, 1, scaled * xin[rows, :].astype(F32))
 
-    loop(TILES, cross)
+    for c in range(3):
+        sib_part(k, c, ch).wait_recv()
+        when(k > 0, functools.partial(run_arrival, k, c))
+        when(k < 3, functools.partial(run_arrival, 4 + k, c))
+        loop(2 * c + 2, cross, 2 * c)
     send_sums(1)
-    await_sums(0)
+
+    def prepare(i):
+        rows = aligned(i, LEN)
+        inverse = column(fin[0, pl.ds(i, 1), :])
+        acc[rows, :] = grads[ch, rows, :].astype(F32) + inverse * acc[rows, :]
+        mixed[rows, :] = xin[rows, :].astype(F32) * (inverse * inverse * inverse)
+
+    loop(TILES, prepare)
     await_sums(1)
-
-    def total(which):
-        full = sums[which, 0]
-        for src in range(1, 8):
-            full = full + sums[which, src]
-        return full
-
-    fin[0] = lax.rsqrt(total(0) / D + EPS)
     fin[1] = total(1) / D
-
-    def column(row):
-        tall = jnp.broadcast_to(row, (128, 128)).T
-        return jnp.concatenate([tall] * BLOCKS, axis=1)
 
     def finish(i):
         rows = aligned(i, LEN)
-        inverse = column(fin[0, pl.ds(i, 1), :])
-        crossed = column(fin[1, pl.ds(i, 1), :])
-        outv[rows, :] = (
-            grads[ch, rows, :].astype(F32)
-            + inverse * acc[rows, :]
-            - xin[rows, :].astype(F32) * (inverse * inverse * inverse) * crossed
-        ).astype(BF16)
+        outv[rows, :] = (acc[rows, :] - mixed[rows, :] * column(fin[1, pl.ds(i, 1), :])).astype(BF16)
 
     loop(TILES, finish)
     store = local(outv, out_h, 7)
@@ -553,10 +561,13 @@
                 sib_copy(src_k, step).wait_send()
 
             when(have, drain)
-    for j in order:
-        remote(parts.at[0, j], sibs.at[j], ss.at[j], sr.at[j], ctx, sib).wait_send()
-        when(j > k, chain_copy(j, 0).wait_send)
-        when(j < k, chain_copy(j, 1).wait_send)
+    def drain_chain(n):
+        j, c = target(n // 3), n % 3
+        sib_part(j, c, sib).wait_send()
+        when(j > k, chain_copy(j, c, 0).wait_send)
+        when(j < k, chain_copy(j, c, 1).wait_send)
+
+    loop(12, drain_chain)
     store.wait()
 
 
@@ -608,10 +619,10 @@
             dma((4,)),
             dma((2, 8)),
             dma((2, 8)),
-            dma((4,)),
-            dma((4,)),
-            dma((4,)),
-            dma((8,)),
+            dma((4, 3)),
+            dma((4, 3)),
+            dma((4, 3)),
+            dma((8, 3)),
         ],
         compiler_params=pltpu.CompilerParams(
             collective_id=0, has_side_effects=True, vmem_limit_bytes=66 * 1024 * 1000

time: 214 us -> 175 us (0.82)
  Pallas kernels: 211 us -> 170 us
    pallas_call x1, Pallas kernels: 211 us -> 170 us  [on_device(): pl.pallas_call(kernel, out_shape=jax.ShapeDtypeStruct((TOK, CH), BF16), i...]
where the time goes in v2:
time: 175 us; the launch traced here: 174 us
  Pallas kernels  170 us (97%)
  local copies, waits for them, and re-layouts  3.32 us (2%)
    pallas_call x1, Pallas kernels, on_device(): pl.pallas_call(kernel, out_shape=jax.ShapeDtypeStruct((TOK, CH), BF16), i...  170 us

profile of v2, /device:TPU:1, one launch (start us, length us, event | category | flops | bytes accessed | tf_op | source)
XLA Modules:
  0.0 173.6 jit_solution(12905756254621514318)
XLA Ops:
  0.0 0.0 copy-start
  0.0 0.7 copy-done
  0.7 0.6 reshape.3.gain_v
  1.3 170.2 %shard_map.100 = bf16[768,512]{1,0:T(8,128)(2,1)} custom-call(bf16[768,512]{1,0:T(8,128)(2,1)} %go_h.1, bf16[768,512]{1,0:T(8,128)(2,1)} %x_h.1, bf16[1,512]{1,0:T(2,128)(2,1)} %reshape.3.gain_v, bf16[768,512]{1,0:T(8,128)(2,1)} %q_h.1, bf16[768,512]{1,0:T(8,128)(2,1)} %k_h.1, bf16[768,512]{1,0:T(8,128)(2,1)} %v_h.1, bf16[32,128]{1,0:T(8,128)(2,1)} %filt_v.1, ...), custom_call_target="tpu_custom_call" | custom-call | tf_op jit(solution)/shard_map/pallas_call | solution.py:580
  171.5 2.1 %copy.12 = bf16[768,512]{1,0:T(8,128)(2,1)} copy(bf16[768,512]{1,0:T(8,128)(2,1)} %shard_map.100) | data formatting | bytes 1572864
Async XLA Ops:
  0.0 0.7 copy-start

commit v3 on v2

--- a/solution.py
+++ b/solution.py
@@ -20,6 +20,13 @@
 F32 = jnp.float32
 BF16 = jnp.bfloat16
 NT = (((1,), (1,)), ((), ()))
+SCHEDULE = (
+    "a1", "b1", "a2", "b2", "a3", "b3", "F35", "c0", "a4", "c1", "b4", "d0",
+    "a5", "c2", "Z01", "d1", "c3", "Z02", "d2", "c4", "T", "Z03", "d3", "F12",
+    "F0", "Z11", "c5", "Z12", "d4", "c6", "a6", "b5", "M0", "Z13", "Z21", "B01",
+    "Z22", "M1", "d5", "Z23", "B23", "M2", "B44", "b6", "B5", "d6",
+)
+STRIPS = ((0, 384), (384, 256), (640, 128))
 
 
 def aligned(index, size):
@@ -212,59 +219,53 @@
             if event <= 5:
                 go(ring_copy(w, zz, quarter, event))
 
-    def line_copy(src_k, side, step):
+    def strip(t):
+        return pl.ds(*STRIPS[t])
+
+    def line_copy(src_k, side, step, t):
         d = 2 * src_k + core
         to = (ch + 2) % 8 if side == 0 else (ch + 6) % 8
-        src = go_h if step == 0 else grads.at[d]
-        return remote(src, grads.at[d], ags.at[side, step], agr.at[src_k], ctx, to)
-
-    def sib_copy(src_k, step):
-        d = 2 * src_k + core
-        src = go_h if step == 0 else grads.at[d]
-        return remote(src, grads.at[d], bs.at[src_k], br.at[src_k], ctx, sib)
-
-    def line_relay(step):
-        for side, src_k, have, more in (
-            (0, k - step, k >= step, k < 3),
-            (1, k + step, k + step <= 3, k > 0),
-        ):
-            def relay(side=side, src_k=src_k, more=more):
-                d = 2 * src_k + core
-                remote(grads.at[d], grads.at[d], ags.at[side, step], agr.at[src_k], ctx, ch).wait_recv()
+        dst = grads.at[d, strip(t)]
+        src = go_h.at[strip(t)] if step == 0 else dst
+        return remote(src, dst, ags.at[side, step, t], agr.at[src_k, t], ctx, to)
+
+    def sib_copy(src_k, step, t):
+        dst = grads.at[2 * src_k + core, strip(t)]
+        src = go_h.at[strip(t)] if step == 0 else dst
+        return remote(src, dst, bs.at[src_k, t], br.at[src_k, t], ctx, sib)
+
+    sides = ((0, k, k < 3), (1, 3 - k, k > 0))
+
+    def line_relay(t, step):
+        for side, behind, more in sides:
+            src_k = k - step + 2 * step * side
+
+            def relay(side=side, behind=behind, more=more, src_k=src_k):
+                dst = grads.at[2 * src_k + core, strip(t)]
+                remote(dst, dst, ags.at[side, step, t], agr.at[src_k, t], ctx, ch).wait_recv()
                 if step < 3:
-                    pl.when(more)(line_copy(src_k, side, step).start)
-                sib_copy(src_k, step).start()
-
-            when(have, relay)
-
-    def multiply(d):
-        zi, yi = d // 4, d % 4
-        wide = jnp.concatenate([ows[zi, yi, xi] for xi in range(4)], axis=1)
-
-        def rows_of(m):
-            rows = aligned(m, 256)
+                    pl.when(more)(line_copy(src_k, side, step, t).start)
+                sib_copy(src_k, step, t).start()
+                if t < 2:
+                    pl.when(more & (behind == step))(line_copy(k, side, 0, t + 1).start)
+
+            when(behind >= step, relay)
+
+    def multiply(t):
+        rows = strip(t)
+        for src_k in range(4):
+            dst = grads.at[2 * src_k + 1 - core, rows]
+            remote(dst, dst, bs.at[src_k, t], br.at[src_k, t], ctx, ch).wait_recv()
+
+        def one(i):
+            d = (ch + i) % 8
+            zi, yi = d // 4, d % 4
+            wide = jnp.concatenate([ows[zi, yi, xi] for xi in range(4)], axis=1)
             acc[rows, :] = acc[rows, :] + lax.dot_general(
                 grads[d, rows, :], wide, NT, preferred_element_type=F32
             )
 
-        loop(3, rows_of)
-
-    def line_multiply(step):
-        def one(index):
-            side, other = index // 2, index % 2
-            src_k = k - step + 2 * step * side
-
-            def act():
-                def await_sibling():
-                    d = 2 * src_k + 1 - core
-                    remote(grads.at[d], grads.at[d], bs.at[src_k], br.at[src_k], ctx, ch).wait_recv()
-
-                when(other == 1, await_sibling)
-                multiply(2 * src_k + core + other * (1 - 2 * core))
-
-            when((src_k >= 0) & (src_k <= 3), act)
-
-        loop(4, one)
+        loop(8, one)
 
     go(remote(docs.at[0], docs.at[1], hs.at[0], hr.at[0], up, ch))
     go(remote(docs.at[0], docs.at[2], hs.at[1], hr.at[1], down, ch))
@@ -273,9 +274,12 @@
     go(remote(prod.at[pl.ds(TOK, LEN), :], prod.at[pl.ds(0, LEN), :], hs.at[2], hr.at[2], up, ch))
     go(swap_copy(0))
     go(swap_copy(1))
-    go(line_copy(k, 0, 0), k < 3)
-    go(line_copy(k, 1, 0), k > 0)
-    go(sib_copy(k, 0))
+    for side, behind, more in sides:
+        when(more, line_copy(k, side, 0, 0).start)
+        for t in (1, 2):
+            when(behind == 0, line_copy(k, side, 0, t).start)
+    for t in range(3):
+        go(sib_copy(k, 0, t))
 
     def send_sums(which):
         for step in range(1, 8):
@@ -325,65 +329,20 @@
 
         loop(BLOCKS, one)
 
-    for event in (1, 2, 3):
-        weights(0, 0, event)
-        weights(1, 0, event)
-    loop(TILES, forward, 3)
-    weights(0, 1, 0)
-    weights(0, 0, 4)
-    weights(0, 1, 1)
-    weights(1, 0, 4)
-    weights(1, 1, 0)
-    weights(0, 0, 5)
-    weights(0, 1, 2)
-    line_relay(1)
-    weights(1, 1, 1)
-    weights(0, 1, 3)
-    weights(1, 1, 2)
-    weights(0, 1, 4)
-    build(1, tabb)
-    weights(1, 1, 3)
-    loop(3, forward, 1)
-    remote(prod.at[pl.ds(TOK, LEN), :], prod.at[pl.ds(0, LEN), :], hs.at[2], hr.at[2], ctx, ch).wait_recv()
-    remote(docs.at[0], docs.at[1], hs.at[0], hr.at[0], ctx, ch).wait_recv()
-    forward(0)
-    line_relay(2)
-    weights(0, 1, 5)
-    weights(1, 1, 4)
-    weights(0, 1, 6)
-    weights(0, 0, 6)
-    loads[4].wait()
-    acc[...] = jnp.zeros((TOK, CH), F32)
-    multiply(2 * k + core)
-    remote(grads.at[sib], grads.at[sib], bs.at[k], br.at[k], ctx, ch).wait_recv()
-    multiply(sib)
-    weights(1, 0, 5)
-    line_multiply(1)
-    line_relay(3)
-    line_multiply(2)
-    weights(1, 1, 5)
-    line_multiply(3)
-
-    loads[6].wait()
-
     def gates(i):
         rows = aligned(i, LEN)
         mix = acc[rows, :]
         wg[rows, :] = (mix * qry[rows, :].astype(F32)).astype(BF16)
         stk[0, rows, :] = (mix * mixed[rows, :]).astype(BF16)
 
-    loop(1, gates)
-    go(remote(wg.at[pl.ds(0, LEN), :], wg.at[pl.ds(TOK, LEN), :], hs.at[3], hr.at[3], down, ch))
-    loop(TILES, gates, 1)
-    remote(docs.at[0], docs.at[2], hs.at[1], hr.at[1], ctx, ch).wait_recv()
+    def head_copy(to):
+        return remote(wg.at[pl.ds(0, LEN), :], wg.at[pl.ds(TOK, LEN), :], hs.at[3], hr.at[3], to, ch)
 
     def backward(i):
-        set_mask(
-            row_pos + i * LEN,
-            col_pos + i * LEN,
-            [docs[0, r : r + 1, :] for r in range(DOCS)]
-            + [docs[2, r : r + 1, :] + TOK for r in range(DOCS)],
-        )
+        firsts = [docs[0, r : r + 1, :] for r in range(DOCS)]
+        if isinstance(i, int):
+            firsts += [docs[2, r : r + 1, :] + TOK for r in range(DOCS)]
+        set_mask(row_pos + i * LEN, col_pos + i * LEN, firsts)
 
         def one(b):
             rows, lanes = aligned(i, LEN), aligned(b, 128)
@@ -392,12 +351,6 @@
             stk[2, rows, lanes] = (conv * key[rows, lanes].astype(F32)).astype(BF16)
 
         loop(BLOCKS, one)
-
-    loop(TILES - 1, backward)
-    weights(1, 0, 6)
-    remote(wg.at[pl.ds(0, LEN), :], wg.at[pl.ds(TOK, LEN), :], hs.at[3], hr.at[3], ctx, ch).wait_recv()
-    loop(TILES, backward, TILES - 1)
-    weights(1, 1, 6)
 
     order = [3 * (1 - k // 2), (2 + 3 * k) % 5, 1 + k % 2, k]
 
@@ -483,9 +436,46 @@
     when(k == 0, clear(0))
     when(k == 3, clear(7))
 
+    loads[4].wait()
+    loads[6].wait()
+    acc[...] = jnp.zeros((TOK, CH), F32)
+
+    def act(name):
+        kind, args = name[0], [int(c) for c in name[1:]]
+        if kind in "abcd":
+            weights("abcd".index(kind) % 2, "abcd".index(kind) // 2, args[0])
+        elif kind == "Z":
+            line_relay(*args)
+        elif kind == "M":
+            multiply(args[0])
+            first, count = STRIPS[args[0]]
+            loop((first + count) // LEN, gates, first // LEN)
+            if args[0] == 0:
+                go(head_copy(down))
+        elif kind == "F":
+            if args[0] == 0:
+                halo.wait_recv()
+                remote(docs.at[0], docs.at[1], hs.at[0], hr.at[0], ctx, ch).wait_recv()
+                forward(0)
+            else:
+                loop(args[1] + 1, forward, args[0])
+        elif kind == "T":
+            build(1, tabb)
+        elif kind == "B":
+            if args[0] == 5:
+                head_copy(ctx).wait_recv()
+                remote(docs.at[0], docs.at[2], hs.at[1], hr.at[1], ctx, ch).wait_recv()
+                backward(5)
+            else:
+                loop(args[1] + 1, backward, args[0])
+
+    halo = remote(prod.at[pl.ds(TOK, LEN), :], prod.at[pl.ds(0, LEN), :], hs.at[2], hr.at[2], ctx, ch)
+    for name in SCHEDULE:
+        act(name)
+
     def job(n):
         partials(target(n // 3), n % 3)
-        done = n - 2
+        done = n - 1
 
         def behind():
             forward_sum(target(done // 3), done % 3)
@@ -550,19 +540,21 @@
             copy.wait_send()
         else:
             pl.when(cond)(copy.wait_send)
-    for step in (1, 2, 3):
-        for side, src_k, have, more in (
-            (0, k - step, k >= step, k < 3),
-            (1, k + step, k + step <= 3, k > 0),
-        ):
-            def drain(side=side, src_k=src_k, more=more):
-                if step < 3:
-                    pl.when(more)(line_copy(src_k, side, step).wait_send)
-                sib_copy(src_k, step).wait_send()
-
-            when(have, drain)
+    for t in range(3):
+        for side, behind, more in sides:
+            when(more, line_copy(k, side, 0, t).wait_send)
+            for step in (1, 2, 3):
+                src_k = k - step + 2 * step * side
+
+                def drain(side=side, more=more, src_k=src_k, step=step):
+                    if step < 3:
+                        pl.when(more)(line_copy(src_k, side, step, t).wait_send)
+                    sib_copy(src_k, step, t).wait_send()
+
+                when(behind >= step, drain)
+
     def drain_chain(n):
-        j, c = target(n // 3), n % 3
+        j, c = n // 3, n % 3
         sib_part(j, c, sib).wait_send()
         when(j > k, chain_copy(j, c, 0).wait_send)
         when(j < k, chain_copy(j, c, 1).wait_send)
@@ -607,10 +599,10 @@
             pltpu.VMEM((2, 8, 128), F32),
             pltpu.VMEM((TOK, CH), BF16),
             dma((8,)),
-            dma((2, 3)),
-            dma((4,)),
-            dma((4,)),
-            dma((4,)),
+            dma((2, 3, 3)),
+            dma((4, 3)),
+            dma((4, 3)),
+            dma((4, 3)),
             dma((2,)),
             dma((2,)),
             dma((2, 2, 4, 6)),

time: 175 us -> 173 us (0.989)
  no operation moved by 1% of the time
where the time goes in v3:
time: 173 us
  Pallas kernels  170 us (98%)
  local copies, waits for them, and re-layouts  3.32 us (2%)
    pallas_call x1, Pallas kernels, on_device(): pl.pallas_call(kernel, out_shape=jax.ShapeDtypeStruct((TOK, CH), BF16), i...  170 us

profile of v3, /device:TPU:1, one launch (start us, length us, event | category | flops | bytes accessed | tf_op | source)
XLA Modules:
  0.0 173.1 jit_solution(6797280356651551231)
XLA Ops:
  0.0 0.0 copy-start
  0.0 0.7 copy-done
  0.7 0.6 reshape.3.gain_v
  1.3 169.8 %shard_map.100 = bf16[768,512]{1,0:T(8,128)(2,1)} custom-call(bf16[768,512]{1,0:T(8,128)(2,1)} %go_h.1, bf16[768,512]{1,0:T(8,128)(2,1)} %x_h.1, bf16[1,512]{1,0:T(2,128)(2,1)} %reshape.3.gain_v, bf16[768,512]{1,0:T(8,128)(2,1)} %q_h.1, bf16[768,512]{1,0:T(8,128)(2,1)} %k_h.1, bf16[768,512]{1,0:T(8,128)(2,1)} %v_h.1, bf16[32,128]{1,0:T(8,128)(2,1)} %filt_v.1, ...), custom_call_target="tpu_custom_call" | custom-call | tf_op jit(solution)/shard_map/pallas_call | solution.py:572
  171.0 2.1 %copy.12 = bf16[768,512]{1,0:T(8,128)(2,1)} copy(bf16[768,512]{1,0:T(8,128)(2,1)} %shard_map.100) | data formatting | bytes 1572864
Async XLA Ops:
  0.0 0.7 copy-start
